TPU v7x, 32 devices: a whole 2x2x4 slice. The times are simulated.
32 devices in a mesh: parts: 2 (over y), seq: 4 (over z), head: 2 (over x), fsdp: 2 (over core).
Axes of the slice: x: 2, y: 2, z: 4, core: 2. Of those that a mesh axis runs over, the one named last changes fastest.
Arguments:
- frames: bfloat16 [2048, 1024], P(('parts', 'seq', 'head', 'fsdp')), parts along dimension 0, may hold values from -24 to 24
- length: int32 [2], P('parts'), parts along dimension 0, may hold values from 512 to 1024
- ln1_gain: float32 [1024], replicated, may hold values from 0.1 to 1.9
- w_query: bfloat16 [1024, 1024], P('seq', ('head', 'fsdp')), may hold values from -0.2 to 0.2
- w_key: bfloat16 [1024, 1024], P('seq', ('head', 'fsdp')), may hold values from -3 to 3
- w_value: bfloat16 [1024, 1024], P('seq', ('head', 'fsdp')), may hold values from -0.375 to 0.375
- w_out: bfloat16 [1024, 1024], P(('head', 'fsdp'), 'seq'), may hold values from -0.1875 to 0.1875
- ln2_gain: float32 [1024], replicated, may hold values from 0.1 to 1.9
- pw1_value: bfloat16 [1024, 1024], P('seq', ('head', 'fsdp')), may hold values from -0.1875 to 0.1875
- pw1_gate: bfloat16 [1024, 1024], P('seq', ('head', 'fsdp')), may hold values from -0.375 to 0.375
- depth_kernel: float32 [9, 1024], P(None, ('head', 'fsdp')), may hold values from -2 to 2
- bn_scale: float32 [1024], P(('head', 'fsdp')), may hold values from 0.1 to 1.9
- bn_shift: float32 [1024], P(('head', 'fsdp')), may hold values from -3 to 3
- pw2: bfloat16 [1024, 1024], P(('head', 'fsdp'), 'seq'), may hold values from -0.1875 to 0.1875
Outputs:
- encoded: bfloat16 [2048, 1024], P(('parts', 'seq', 'head', 'fsdp')), parts along dimension 0
There are 2 independent parts, one for each index of `parts`. A program takes and returns all parts, laid end to end along the dimension named above; an argument that names none is the same for every part. Nothing has to cross between parts.
All inputs are finite; a program needn't handle non-finite values.
Results may differ from a plain program's by a relative error of at most 0.012.
The roundings to bfloat16 on the way count: a program that leaves them out, or rounds other values in their place, can miss the bound.
Values may be sent and summed in bfloat16 or wider, within the bound.
No kernel may reach another device: no remote copies, remote signals or barrier semaphores. Data moves between devices by JAX's collectives and lax.ppermute only.
A program may use at most 64 MiB of HBM per device.

v0:
```python
import math
import jax
import jax.numpy as jnp
from jax import lax
from jax.sharding import PartitionSpec as P

KERNEL = 9
HD = 128


def with_halo(block, sides, width):
    for axis, dim in sides:
        count = lax.axis_size(axis)
        forward = [(i, i + 1) for i in range(count - 1)]
        backward = [(target, source) for source, target in forward]
        low = lax.ppermute(
            lax.slice_in_dim(block, block.shape[dim] - width, None, axis=dim), axis, forward
        )
        high = lax.ppermute(lax.slice_in_dim(block, 0, width, axis=dim), axis, backward)
        block = jnp.concatenate([low, block, high], axis=dim)
    return block


def layer_norm(values_in, gain_vec):
    center = jnp.mean(values_in, axis=-1, keepdims=True)
    shifted = values_in - center
    spread = jnp.mean(shifted * shifted, axis=-1, keepdims=True)
    return shifted * lax.rsqrt(spread + 1e-05) * gain_vec


def shards(
    frames,
    length,
    ln1_gain,
    w_query,
    w_key,
    w_value,
    w_out,
    ln2_gain,
    pw1_value,
    pw1_gate,
    depth_kernel,
    bn_scale,
    bn_shift,
    pw2,
):
    group_size = lax.axis_size(("head", "fsdp"))
    my_rows = frames.shape[0]
    block_rows = my_rows * group_size
    head_cols = w_query.shape[1]
    heads_here = head_cols // HD
    seq_start = lax.axis_index("seq") * block_rows
    valid_len = length[0]
    score_scale = 1.0 / math.sqrt(HD)
    full_query, full_key, full_value, value_cols, gate_cols = (
        lax.all_gather(w_query, "seq", axis=0, tiled=True),
        lax.all_gather(w_key, "seq", axis=0, tiled=True),
        lax.all_gather(w_value, "seq", axis=0, tiled=True),
        lax.all_gather(pw1_value, "seq", axis=0, tiled=True),
        lax.all_gather(pw1_gate, "seq", axis=0, tiled=True),
    )
    out_rows, down_rows = (
        lax.all_gather(w_out, "seq", axis=1, tiled=True),
        lax.all_gather(pw2, "seq", axis=1, tiled=True),
    )
    projector = jnp.concatenate((full_query, full_key, full_value), axis=1)
    source = frames.astype(jnp.float32)
    normed = layer_norm(source, ln1_gain).astype(jnp.bfloat16)
    projected = jnp.dot(
        lax.all_gather(normed, ("head", "fsdp"), axis=0, tiled=True),
        projector,
        preferred_element_type=jnp.float32,
    ).astype(jnp.bfloat16)
    queries = projected[:, :head_cols].reshape(block_rows, heads_here, HD)
    keys_here = projected[:, head_cols : 2 * head_cols]
    values_here = projected[:, 2 * head_cols :]
    initial = (
        jnp.full((heads_here, block_rows), -1e30, jnp.float32),
        jnp.zeros((heads_here, block_rows), jnp.float32),
        jnp.zeros((heads_here, block_rows, HD), jnp.float32),
    )
    key_piece = lax.all_gather(keys_here, "seq", axis=0, tiled=True)
    value_piece = lax.all_gather(values_here, "seq", axis=0, tiled=True)
    row_count = key_piece.shape[0]
    block_size = math.gcd(row_count, 512)
    block_count = row_count // block_size
    key_blocks = key_piece.reshape(block_count, block_size, heads_here, HD)
    value_blocks = value_piece.reshape(block_count, block_size, heads_here, HD)
    places = jnp.arange(row_count, dtype=jnp.int32).reshape(block_count, block_size)

    def advance(inner_state, block_item):
        key_block, value_block, place = block_item
        peak_score, weight_sum, weighted = inner_state
        scores = (
            jnp.einsum("qhd,khd->hqk", queries, key_block, preferred_element_type=jnp.float32)
            * score_scale
        )
        scores = jnp.where((place < valid_len)[None, None, :], scores, -jnp.inf)
        new_peak = jnp.maximum(peak_score, jnp.max(scores, axis=2))
        factor = jnp.exp(peak_score - new_peak)
        weights = jnp.exp(scores - new_peak[:, :, None])
        weight_sum = weight_sum * factor + jnp.sum(weights, axis=2)
        weighted = weighted * factor[:, :, None] + jnp.einsum(
            "hqk,khd->hqd",
            weights.astype(jnp.bfloat16),
            value_block,
            preferred_element_type=jnp.float32,
        )
        return ((new_peak, weight_sum, weighted), None)

    result, unused = lax.scan(advance, initial, (key_blocks, value_blocks, places))
    peak_score, weight_sum, weighted = result
    context = (
        (weighted / weight_sum[:, :, None])
        .astype(jnp.bfloat16)
        .transpose(1, 0, 2)
        .reshape(block_rows, head_cols)
    )
    attended = lax.psum_scatter(
        jnp.dot(context, out_rows, preferred_element_type=jnp.float32).astype(jnp.bfloat16),
        ("head", "fsdp"),
        scatter_dimension=0,
        tiled=True,
    ).astype(jnp.float32)
    middle = source + attended
    normed_two = layer_norm(middle, ln2_gain).astype(jnp.bfloat16)
    piece = lax.all_gather(normed_two, ("head", "fsdp"), axis=0, tiled=True)
    value_part = jnp.dot(piece, value_cols, preferred_element_type=jnp.float32)
    gate_part = jnp.dot(piece, gate_cols, preferred_element_type=jnp.float32)
    places = seq_start + jnp.arange(piece.shape[0], dtype=jnp.int32)
    gated_rows = jnp.where(
        (places < valid_len)[:, None], value_part * jax.nn.sigmoid(gate_part), 0.0
    ).astype(jnp.bfloat16)
    rim_width = (KERNEL - 1) // 2
    padded = with_halo(gated_rows, (("seq", 0),), rim_width).astype(jnp.float32)
    depth_sum = depth_kernel[0] * padded[0:block_rows]
    for offset in range(1, KERNEL):
        depth_sum = depth_sum + depth_kernel[offset] * padded[offset : offset + block_rows]
    shifted = depth_sum * bn_scale + bn_shift
    active = (shifted * jax.nn.sigmoid(shifted)).astype(jnp.bfloat16)
    conv_part = lax.psum_scatter(
        jnp.dot(active, down_rows, preferred_element_type=jnp.float32).astype(jnp.bfloat16),
        ("head", "fsdp"),
        scatter_dimension=0,
        tiled=True,
    ).astype(jnp.float32)
    return (middle + conv_part).astype(jnp.bfloat16)


def solution(mesh):
    in_specs = (
        P(("parts", "seq", "head", "fsdp"), None),
        P("parts"),
        P(),
        P("seq", ("head", "fsdp")),
        P("seq", ("head", "fsdp")),
        P("seq", ("head", "fsdp")),
        P(("head", "fsdp"), "seq"),
        P(),
        P("seq", ("head", "fsdp")),
        P("seq", ("head", "fsdp")),
        P(None, ("head", "fsdp")),
        P(("head", "fsdp")),
        P(("head", "fsdp")),
        P(("head", "fsdp"), "seq"),
    )
    out_specs = P(("parts", "seq", "head", "fsdp"), None)
    return jax.shard_map(shards, mesh=mesh, in_specs=in_specs, out_specs=out_specs, check_vma=False)
```

profile of v0, /device:TPU:0, one launch (start us, length us, event | category | flops | bytes accessed | tf_op | source)
XLA Modules:
  0.0 217.0 jit_solution(8973462292048037482)
XLA Ops:
  6.6 1.1 convert_reduce_fusion
  7.7 1.1 fusion.24
  8.8 1.0 fusion.26
  9.8 0.0 copy-start.4
  9.8 8.8 %all_gather.33 = bf16[256,1024]{1,0:T(8,128)(2,1)S(1)} all-gather(bf16[64,1024]{1,0:T(8,128)(2,1)S(1)} %fusion.26), channel_id=1, replica_groups=mesh['parts'=2,'seq'=4,'head'=2,'fsdp'=2] {'head','fsdp'}, dimensions={0}, use_global_device_ids=true | all-gather | bytes 655360 | tf_op jit(solution)/shard_map/all_gather | solution.py:70
  18.6 16.3 %all_gather.34 = bf16[1024,256]{1,0:T(8,128)(2,1)S(1)} all-gather(bf16[256,256]{1,0:T(8,128)(2,1)S(1)} %copy-done.2), channel_id=1, replica_groups=mesh['parts'=2,'seq'=4,'head'=2,'fsdp'=2] {'seq'}, dimensions={0}, use_global_device_ids=true | all-gather | bytes 655360 | tf_op jit(solution)/shard_map/all_gather | solution.py:56
  34.9 15.9 %all_gather.35 = bf16[1024,256]{1,0:T(8,128)(2,1)S(1)} all-gather(bf16[256,256]{1,0:T(8,128)(2,1)S(1)} %copy-done.3), channel_id=1, replica_groups=mesh['parts'=2,'seq'=4,'head'=2,'fsdp'=2] {'seq'}, dimensions={0}, use_global_device_ids=true | all-gather | bytes 655360 | tf_op jit(solution)/shard_map/all_gather | solution.py:57
  50.8 16.1 %all_gather.36 = bf16[1024,256]{1,0:T(8,128)(2,1)S(1)} all-gather(bf16[256,256]{1,0:T(8,128)(2,1)S(1)} %copy-done.4), channel_id=1, replica_groups=mesh['parts'=2,'seq'=4,'head'=2,'fsdp'=2] {'seq'}, dimensions={0}, use_global_device_ids=true | all-gather | bytes 655360 | tf_op jit(solution)/shard_map/all_gather | solution.py:58
  67.0 0.6 fusion.14
  67.6 14.8 %all_gather.37 = bf16[1024,256]{1,0:T(8,128)(2,1)S(1)} all-gather(bf16[256,256]{1,0:T(8,128)(2,1)S(1)} %get-tuple-element.129), channel_id=1, replica_groups=mesh['parts'=2,'seq'=4,'head'=2,'fsdp'=2] {'seq'}, dimensions={0}, use_global_device_ids=true | all-gather | bytes 655360 | tf_op jit(solution)/shard_map/all_gather | solution.py:82
  82.4 0.1 reshape.65
  82.5 16.1 %all_gather.38 = bf16[1024,256]{1,0:T(8,128)(2,1)S(1)} all-gather(bf16[256,256]{1,0:T(8,128)(2,1)S(1)} %get-tuple-element.127), channel_id=1, replica_groups=mesh['parts'=2,'seq'=4,'head'=2,'fsdp'=2] {'seq'}, dimensions={0}, use_global_device_ids=true | all-gather | bytes 655360 | tf_op jit(solution)/shard_map/all_gather | solution.py:83
  98.6 0.1 reshape.67
  98.7 0.0 copy-start.5
  98.8 4.0 %while.15 = (s32[]{:T(128)}, f32[2,256]{1,0:T(2,128)S(1)}, f32[2,256]{1,0:T(2,128)S(1)}, f32[2,256,128]{2,1,0:T(8,128)S(1)}, s32[2,512]{1,0:T(2,128)S(1)}, /*ind...) while((s32[]{:T(128)}, f32[2,256]{1,0:T(2,128)S(1)}, ...), condition=%wide.region_5.6_spmd.clone, body=%wide.region_2.5_spmd.clone.sunk | while | flops 136252416 | bytes 5409925 | solution.py:111
  98.8 0.4 constant_dynamic-slice_fusion.3
  99.1 0.7 compare_reduce_fusion.2
  99.8 0.3 fusion.61
  100.1 0.2 fusion.63
  100.3 0.4 convolution_add_fusion.2
  100.8 0.4 constant_dynamic-slice_fusion.3
  101.2 0.7 compare_reduce_fusion.2
  101.8 0.3 fusion.61
  102.2 0.2 fusion.63
  102.4 0.4 convolution_add_fusion.2
  102.8 0.1 copy.23
  103.0 15.8 %all_gather.39 = bf16[256,1024]{1,0:T(8,128)(2,1)S(1)} all-gather(bf16[256,256]{1,0:T(8,128)(2,1)S(1)} %copy-done.5), channel_id=1, replica_groups=mesh['parts'=2,'seq'=4,'head'=2,'fsdp'=2] {'seq'}, dimensions={1}, use_global_device_ids=true | all-gather | bytes 655360 | tf_op jit(solution)/shard_map/all_gather | solution.py:63
  118.8 1.1 convolution_convert_fusion.1
  119.9 0.0 reduce-scatter.3.cloned.1.call-update
  120.0 0.0 reduce-scatter.5.cloned.1.call-start
  120.7 15.6 %all_gather.42 = bf16[1024,256]{1,0:T(8,128)(2,1)S(1)} all-gather(bf16[256,256]{1,0:T(8,128)(2,1)S(1)} %copy-done.6), channel_id=1, replica_groups=mesh['parts'=2,'seq'=4,'head'=2,'fsdp'=2] {'seq'}, dimensions={0}, use_global_device_ids=true | all-gather | bytes 655360 | tf_op jit(solution)/shard_map/all_gather | solution.py:60
  136.2 15.0 %all_gather.41 = bf16[1024,256]{1,0:T(8,128)(2,1)S(1)} all-gather(bf16[256,256]{1,0:T(8,128)(2,1)S(1)} %copy-done.7), channel_id=1, replica_groups=mesh['parts'=2,'seq'=4,'head'=2,'fsdp'=2] {'seq'}, dimensions={0}, use_global_device_ids=true | all-gather | bytes 655360 | tf_op jit(solution)/shard_map/all_gather | solution.py:59
  151.2 0.0 reduce-scatter.3.cloned.1.call-done
  151.3 1.0 fusion.37
  152.3 1.1 multiply_reduce_fusion
  153.5 1.0 multiply_convert_fusion.1
  154.5 6.8 %all_gather.40 = bf16[256,1024]{1,0:T(8,128)(2,1)S(1)} all-gather(bf16[64,1024]{1,0:T(8,128)(2,1)S(1)} %multiply_convert_fusion.1), channel_id=1, replica_groups=mesh['parts'=2,'seq'=4,'head'=2,'fsdp'=2] {'head','fsdp'}, dimensions={0}, use_global_device_ids=true | all-gather | bytes 655360 | tf_op jit(solution)/shard_map/all_gather | solution.py:127
  161.3 0.3 fusion.19
  161.6 0.0 copy-start.11
  161.6 0.0 copy-start.12
  161.6 0.3 fusion.21
  161.9 3.9 %collective-permute-start = (bf16[4,256]{1,0:T(4,128)(2,1)S(1)}, bf16[4,256]{1,0:T(4,128)(2,1)S(1)}, u32[]{:S(2)}, u32[]{:S(2)}) collective-permute-start(bf16[4,256]{1,0:T(4,128)(2,1)S(1)} %get-tuple-element.130), channel_id=1, source_target_pairs={{0,4},{4,8},{8,12},{1,5},{5,9},{9,13},{2,6},{6,10},{10,14},{3,7},{... | collective-permute-start | bytes 6152 | tf_op jit(solution)/shard_map/ppermute | solution.py:16
  165.8 1.3 collective-permute-start.1
  167.2 16.9 %all_gather.43 = bf16[256,1024]{1,0:T(8,128)(2,1)S(1)} all-gather(bf16[256,256]{1,0:T(8,128)(2,1)S(1)} %copy-done.8), channel_id=1, replica_groups=mesh['parts'=2,'seq'=4,'head'=2,'fsdp'=2] {'seq'}, dimensions={1}, use_global_device_ids=true | all-gather | bytes 655360 | tf_op jit(solution)/shard_map/all_gather | solution.py:64
  184.2 1.4 convolution_convert_fusion
  185.5 0.0 reduce-scatter.5.cloned.1.call-update
  185.5 23.0 %reduce-scatter.5.cloned.1.call-done = bf16[64,1024]{1,0:T(8,128)(2,1)} async-done(((bf16[256,1024]{1,0:T(8,128)(2,1)}), bf16[64,1024]{1,0:T(8,128)(2,1)}) %reduce-scatter.5.cloned.1.call-update) | async-done | bytes 131088 | tf_op jit(solution)/shard_map/reduce_scatter | solution.py:141
  208.5 1.6 add_convert_fusion
  (46 shorter events, 0.3 us)
Async XLA Ops:
  6.5 12.0 %copy-start.2 = (bf16[256,256]{1,0:T(8,128)(2,1)S(1)}, bf16[256,256]{1,0:T(8,128)(2,1)}, u32[]{:S(2)}) copy-start(bf16[256,256]{1,0:T(8,128)(2,1)} %param.19) | copy-start | bytes 393220
  6.5 28.4 %copy-start.3 = (bf16[256,256]{1,0:T(8,128)(2,1)S(1)}, bf16[256,256]{1,0:T(8,128)(2,1)}, u32[]{:S(2)}) copy-start(bf16[256,256]{1,0:T(8,128)(2,1)} %param.20) | copy-start | bytes 393220
  6.5 144.7 %reduce-scatter.3.cloned.1.call-start = ((), (), s32[]{:S(2)}) async-start(), calls=%async_computation.2 | async-start | bytes 655360 | tf_op jit(solution)/shard_map/reduce_scatter | solution.py:119
  9.8 41.0 %copy-start.4 = (bf16[256,256]{1,0:T(8,128)(2,1)S(1)}, bf16[256,256]{1,0:T(8,128)(2,1)}, u32[]{:S(2)}) copy-start(bf16[256,256]{1,0:T(8,128)(2,1)} %param.21) | copy-start | bytes 393220
  98.7 4.2 %copy-start.5 = (bf16[256,256]{1,0:T(8,128)(2,1)S(1)}, bf16[256,256]{1,0:T(8,128)(2,1)}, u32[]{:S(2)}) copy-start(bf16[256,256]{1,0:T(8,128)(2,1)} %param.22) | copy-start | bytes 393220
  118.8 1.9 copy-start.6
  118.8 17.4 %copy-start.7 = (bf16[256,256]{1,0:T(8,128)(2,1)S(1)}, bf16[256,256]{1,0:T(8,128)(2,1)}, u32[]{:S(2)}) copy-start(bf16[256,256]{1,0:T(8,128)(2,1)} %param.24) | copy-start | bytes 393220
  119.9 31.3 %copy-start.9 = (f32[9,256]{1,0:T(8,128)S(1)}, f32[9,256]{1,0:T(8,128)}, u32[]{:S(2)}) copy-start(f32[9,256]{1,0:T(8,128)} %param.26) | copy-start | bytes 27652
  119.9 31.3 %copy-start = (bf16[64,1024]{1,0:T(8,128)(2,1)S(1)}, bf16[64,1024]{1,0:T(8,128)(2,1)}, u32[]{:S(2)}) copy-start(bf16[64,1024]{1,0:T(8,128)(2,1)} %param.16) | copy-start | bytes 393220
  120.0 33.5 %copy-start.10 = (f32[1024]{0:T(1024)S(1)}, f32[1024]{0:T(1024)}, u32[]{:S(2)}) copy-start(f32[1024]{0:T(1024)} %param.23) | copy-start | bytes 12292
  120.0 88.6 %reduce-scatter.5.cloned.1.call-start = ((), (), s32[]{:S(2)}) async-start(), calls=%async_computation.3 | async-start | bytes 655360 | tf_op jit(solution)/shard_map/reduce_scatter | solution.py:141
  161.6 5.6 %copy-start.8 = (bf16[256,256]{1,0:T(8,128)(2,1)S(1)}, bf16[256,256]{1,0:T(8,128)(2,1)}, u32[]{:S(2)}) copy-start(bf16[256,256]{1,0:T(8,128)(2,1)} %param.29) | copy-start | bytes 393220
  161.6 22.5 %copy-start.11 = (f32[256]{0:T(256)S(1)}, f32[256]{0:T(256)}, u32[]{:S(2)}) copy-start(f32[256]{0:T(256)} %param.28) | copy-start | bytes 3076
  161.6 22.5 %copy-start.12 = (f32[256]{0:T(256)S(1)}, f32[256]{0:T(256)}, u32[]{:S(2)}) copy-start(f32[256]{0:T(256)} %param.27) | copy-start | bytes 3076
  161.9 22.2 %collective-permute-start = (bf16[4,256]{1,0:T(4,128)(2,1)S(1)}, bf16[4,256]{1,0:T(4,128)(2,1)S(1)}, u32[]{:S(2)}, u32[]{:S(2)}) collective-permute-start(bf16[4,256]{1,0:T(4,128)(2,1)S(1)} %get-tuple-element.130), channel_id=1, source_target_pairs={{0,4},{4,8},{8,12},{1,5},{5,9},{9,13},{2,6},{6,10},{10,14},{3,7},{... | collective-permute-start | bytes 6152 | tf_op jit(solution)/shard_map/ppermute | solution.py:16
  165.8 18.3 %collective-permute-start.1 = (bf16[4,256]{1,0:T(4,128)(2,1)S(1)}, bf16[4,256]{1,0:T(4,128)(2,1)S(1)}, u32[]{:S(2)}, u32[]{:S(2)}) collective-permute-start(bf16[4,256]{1,0:T(4,128)(2,1)S(1)} %get-tuple-element.131), channel_id=1, source_target_pairs={{4,0},{8,4},{12,8},{5,1},{9,5},{13,9},{6,2},{10,6},{14,10},{7,3},{... | collective-permute-start | bytes 6152 | tf_op jit(solution)/shard_map/ppermute | solution.py:19
  184.2 24.4 %copy-start.1 = (bf16[64,1024]{1,0:T(8,128)(2,1)S(1)}, bf16[64,1024]{1,0:T(8,128)(2,1)}, u32[]{:S(2)}) copy-start(bf16[64,1024]{1,0:T(8,128)(2,1)} %reduce-scatter.3.cloned.1.call-done) | copy-start | bytes 393220
Sparse Core Ops, SparseCore 0:
  120.1 22.2 reduce-scatter.2
  185.7 22.8 reduce-scatter.4
where the time goes:
time: 217 us
  blocking collectives  158 us (73%)
  waiting for transfers between devices  23 us (11%)
  between operations  14.4 us (7%)
  other arithmetic  9.78 us (5%)
  starting transfers between devices  5.23 us (2%)
  matrix products  5.13 us (2%)
    reduce_scatter x1, waiting for transfers between devices, shards(): lax.psum_scatter(jnp.dot(active, down_rows, preferred_element_type=jnp.fl...  23 us
    all_gather x1, blocking collectives, shards(): lax.all_gather(pw2, 'seq', axis=1, tiled=True)  16.9 us
    all_gather x1, blocking collectives, shards(): lax.all_gather(w_query, 'seq', axis=0, tiled=True)  16.3 us
    all_gather x1, blocking collectives, shards(): lax.all_gather(w_value, 'seq', axis=0, tiled=True)  16.1 us
    all_gather x1, blocking collectives, shards(): value_piece = lax.all_gather(values_here, 'seq', axis=0, tiled=True)  16.1 us
    all_gather x1, blocking collectives, shards(): lax.all_gather(w_key, 'seq', axis=0, tiled=True)  15.9 us
    all_gather x1, blocking collectives, shards(): lax.all_gather(w_out, 'seq', axis=1, tiled=True)  15.8 us
    all_gather x1, blocking collectives, shards(): lax.all_gather(pw1_gate, 'seq', axis=0, tiled=True)  15.6 us
  transfers between devices with their start and end apart: 4, of which 1 were waited for; matrix products, arithmetic and copies ran while one was open for 0% of the time, Pallas kernels for 0%

commit v1 on v0

--- a/solution.py
+++ b/solution.py
@@ -6,6 +6,19 @@
 
 KERNEL = 9
 HD = 128
+
+
+def ring_gather(shard, axis, dim):
+    ways = lax.axis_size(axis)
+    up = [(d, (d + 1) % ways) for d in range(ways)]
+    down = [(d, (d - 1) % ways) for d in range(ways)]
+    earlier, later = ([shard], [shard])
+    for _ in range(ways // 2):
+        earlier.append(lax.ppermute(earlier[-1], axis, up))
+    for _ in range((ways - 1) // 2):
+        later.append(lax.ppermute(later[-1], axis, down))
+    line = jnp.concatenate([*earlier[::-1], *later[1:]], axis=dim)
+    return jnp.roll(line, (lax.axis_index(axis) - ways // 2) * shard.shape[dim], axis=dim)
 
 
 def with_halo(block, sides, width):
@@ -55,7 +68,7 @@
     full_query, full_key, full_value, value_cols, gate_cols = (
         lax.all_gather(w_query, "seq", axis=0, tiled=True),
         lax.all_gather(w_key, "seq", axis=0, tiled=True),
-        lax.all_gather(w_value, "seq", axis=0, tiled=True),
+        ring_gather(w_value, "seq", 0),
         lax.all_gather(pw1_value, "seq", axis=0, tiled=True),
         lax.all_gather(pw1_gate, "seq", axis=0, tiled=True),
     )

time: 217 us -> 204 us (0.940)
  blocking collectives: 158 us -> 142 us
  starting transfers between devices: 5.23 us -> 7.74 us
    all_gather x1 -> x0, blocking collectives: 16.1 us -> none  [shards(): lax.all_gather(w_value, 'seq', axis=0, tiled=True)]
    ppermute x0 -> x3, starting transfers between devices: none -> 5.11 us  [the longest x2 3.03 us: ring_gather(): earlier.append(lax.ppermute(earlier[-1], axis, up))]
    ppermute x1, starting transfers between devices: 3.9 us -> 1.29 us  [with_halo(): lax.ppermute(lax.slice_in_dim(block, block.shape[dim] - width, None, axis...]
  transfers between devices with their start and end apart: 4 -> 7, of which waited for: 1 -> 1; matrix products, arithmetic and copies ran while one was open for 0% -> 2% of each run, Pallas kernels for 0% -> 0%
where the time goes in v1:
time: 204 us
  blocking collectives  142 us (70%)
  waiting for transfers between devices  23 us (11%)
  between operations  14.5 us (7%)
  other arithmetic  9.73 us (5%)
  starting transfers between devices  7.74 us (4%)
  matrix products  5.18 us (3%)
    reduce_scatter x1, waiting for transfers between devices, shards(): lax.psum_scatter(jnp.dot(active, down_rows, preferred_element_type=jnp.fl...  23 us
    all_gather x1, blocking collectives, shards(): lax.all_gather(w_out, 'seq', axis=1, tiled=True)  17.4 us
    all_gather x1, blocking collectives, shards(): lax.all_gather(pw2, 'seq', axis=1, tiled=True)  16.6 us
    all_gather x1, blocking collectives, shards(): lax.all_gather(w_key, 'seq', axis=0, tiled=True)  16.2 us
    all_gather x1, blocking collectives, shards(): lax.all_gather(w_query, 'seq', axis=0, tiled=True)  16.1 us
    all_gather x1, blocking collectives, shards(): value_piece = lax.all_gather(values_here, 'seq', axis=0, tiled=True)  16 us
    all_gather x1, blocking collectives, shards(): lax.all_gather(pw1_gate, 'seq', axis=0, tiled=True)  15.9 us
    all_gather x1, blocking collectives, shards(): key_piece = lax.all_gather(keys_here, 'seq', axis=0, tiled=True)  15 us
  transfers between devices with their start and end apart: 7, of which 1 were waited for; matrix products, arithmetic and copies ran while one was open for 2% of the time, Pallas kernels for 0%

profile of v1, /device:TPU:0, one launch (start us, length us, event | category | flops | bytes accessed | tf_op | source)
XLA Modules:
  0.0 203.6 jit_solution(13675703675355699211)
XLA Ops:
  6.5 3.0 %collective-permute-start = (bf16[256,256]{1,0:T(8,128)(2,1)}, bf16[256,256]{1,0:T(8,128)(2,1)S(1)}, u32[]{:S(2)}, u32[]{:S(2)}) collective-permute-start(bf16[256,256]{1,0:T(8,128)(2,1)} %param.21), channel_id=1, source_target_pairs={{0,4},{4,8},{8,12},{12,0},{1,5},{5,9},{9,13},{13,1},{2,6},{6,10},{... | collective-permute-start | bytes 393224 | tf_op jit(solution)/shard_map/ppermute | solution.py:17
  9.6 2.1 %collective-permute-start.2 = (bf16[256,256]{1,0:T(8,128)(2,1)}, bf16[256,256]{1,0:T(8,128)(2,1)S(1)}, u32[]{:S(2)}, u32[]{:S(2)}) collective-permute-start(bf16[256,256]{1,0:T(8,128)(2,1)} %param.21), channel_id=1, source_target_pairs={{0,12},{4,0},{8,4},{12,8},{1,13},{5,1},{9,5},{13,9},{2,14},{6,2},{... | collective-permute-start | bytes 393224 | tf_op jit(solution)/shard_map/ppermute | solution.py:19
  11.6 1.0 convert_reduce_fusion
  12.7 1.1 fusion.24
  13.8 1.0 fusion.26
  14.8 7.5 %all_gather.30 = bf16[256,1024]{1,0:T(8,128)(2,1)S(1)} all-gather(bf16[64,1024]{1,0:T(8,128)(2,1)S(1)} %fusion.26), channel_id=1, replica_groups=mesh['parts'=2,'seq'=4,'head'=2,'fsdp'=2] {'head','fsdp'}, dimensions={0}, use_global_device_ids=true | all-gather | bytes 655360 | tf_op jit(solution)/shard_map/all_gather | solution.py:83
  22.3 16.1 %all_gather.31 = bf16[1024,256]{1,0:T(8,128)(2,1)S(1)} all-gather(bf16[256,256]{1,0:T(8,128)(2,1)S(1)} %copy-done.3), channel_id=1, replica_groups=mesh['parts'=2,'seq'=4,'head'=2,'fsdp'=2] {'seq'}, dimensions={0}, use_global_device_ids=true | all-gather | bytes 655360 | tf_op jit(solution)/shard_map/all_gather | solution.py:69
  38.4 16.2 %all_gather.32 = bf16[1024,256]{1,0:T(8,128)(2,1)S(1)} all-gather(bf16[256,256]{1,0:T(8,128)(2,1)S(1)} %copy-done.4), channel_id=1, replica_groups=mesh['parts'=2,'seq'=4,'head'=2,'fsdp'=2] {'seq'}, dimensions={0}, use_global_device_ids=true | all-gather | bytes 655360 | tf_op jit(solution)/shard_map/all_gather | solution.py:70
  54.6 17.4 %all_gather.35 = bf16[256,1024]{1,0:T(8,128)(2,1)S(1)} all-gather(bf16[256,256]{1,0:T(8,128)(2,1)S(1)} %copy-done.5), channel_id=1, replica_groups=mesh['parts'=2,'seq'=4,'head'=2,'fsdp'=2] {'seq'}, dimensions={1}, use_global_device_ids=true | all-gather | bytes 655360 | tf_op jit(solution)/shard_map/all_gather | solution.py:76
  72.3 0.6 fusion.14
  73.0 15.0 %all_gather.33 = bf16[1024,256]{1,0:T(8,128)(2,1)S(1)} all-gather(bf16[256,256]{1,0:T(8,128)(2,1)S(1)} %get-tuple-element.129), channel_id=1, replica_groups=mesh['parts'=2,'seq'=4,'head'=2,'fsdp'=2] {'seq'}, dimensions={0}, use_global_device_ids=true | all-gather | bytes 655360 | tf_op jit(solution)/shard_map/all_gather | solution.py:95
  87.9 0.1 reshape.65
  88.1 16.0 %all_gather.34 = bf16[1024,256]{1,0:T(8,128)(2,1)S(1)} all-gather(bf16[256,256]{1,0:T(8,128)(2,1)S(1)} %get-tuple-element.127), channel_id=1, replica_groups=mesh['parts'=2,'seq'=4,'head'=2,'fsdp'=2] {'seq'}, dimensions={0}, use_global_device_ids=true | all-gather | bytes 655360 | tf_op jit(solution)/shard_map/all_gather | solution.py:96
  104.1 0.1 reshape.67
  104.2 4.0 %while.15 = (s32[]{:T(128)}, f32[2,256]{1,0:T(2,128)S(1)}, f32[2,256]{1,0:T(2,128)S(1)}, f32[2,256,128]{2,1,0:T(8,128)S(1)}, s32[2,512]{1,0:T(2,128)S(1)}, /*ind...) while((s32[]{:T(128)}, f32[2,256]{1,0:T(2,128)S(1)}, ...), condition=%wide.region_5.6_spmd.clone, body=%wide.region_2.5_spmd.clone.sunk | while | flops 136252416 | bytes 5409925 | solution.py:124
  104.2 0.4 constant_dynamic-slice_fusion.4
  104.6 0.7 compare_reduce_fusion.2
  105.3 0.3 fusion.61
  105.6 0.2 fusion.63
  105.8 0.4 convolution_add_fusion.2
  106.3 0.4 constant_dynamic-slice_fusion.4
  106.6 0.7 compare_reduce_fusion.2
  107.3 0.3 fusion.61
  107.6 0.2 fusion.63
  107.8 0.4 convolution_add_fusion.2
  108.3 0.1 copy.23
  108.4 0.0 copy-start.6
  108.5 0.0 copy-start.7
  108.5 1.1 convolution_convert_fusion.1
  109.6 0.0 reduce-scatter.3.cloned.1.call-update
  109.6 0.0 copy-start.10
  109.6 0.0 reduce-scatter.5.cloned.1.call-start
  110.4 15.9 %all_gather.38 = bf16[1024,256]{1,0:T(8,128)(2,1)S(1)} all-gather(bf16[256,256]{1,0:T(8,128)(2,1)S(1)} %copy-done.6), channel_id=1, replica_groups=mesh['parts'=2,'seq'=4,'head'=2,'fsdp'=2] {'seq'}, dimensions={0}, use_global_device_ids=true | all-gather | bytes 655360 | tf_op jit(solution)/shard_map/all_gather | solution.py:73
  126.3 14.8 %all_gather.37 = bf16[1024,256]{1,0:T(8,128)(2,1)S(1)} all-gather(bf16[256,256]{1,0:T(8,128)(2,1)S(1)} %copy-done.7), channel_id=1, replica_groups=mesh['parts'=2,'seq'=4,'head'=2,'fsdp'=2] {'seq'}, dimensions={0}, use_global_device_ids=true | all-gather | bytes 655360 | tf_op jit(solution)/shard_map/all_gather | solution.py:72
  141.1 0.0 reduce-scatter.3.cloned.1.call-done
  141.1 1.0 fusion.37
  142.2 1.1 multiply_reduce_fusion
  143.3 1.0 multiply_convert_fusion.1
  144.3 6.5 %all_gather.36 = bf16[256,1024]{1,0:T(8,128)(2,1)S(1)} all-gather(bf16[64,1024]{1,0:T(8,128)(2,1)S(1)} %multiply_convert_fusion.1), channel_id=1, replica_groups=mesh['parts'=2,'seq'=4,'head'=2,'fsdp'=2] {'head','fsdp'}, dimensions={0}, use_global_device_ids=true | all-gather | bytes 655360 | tf_op jit(solution)/shard_map/all_gather | solution.py:140
  150.8 0.3 fusion.19
  151.2 0.3 fusion.21
  151.5 1.3 collective-permute-start.3
  152.8 1.3 collective-permute-start.4
  154.1 16.6 %all_gather.39 = bf16[256,1024]{1,0:T(8,128)(2,1)S(1)} all-gather(bf16[256,256]{1,0:T(8,128)(2,1)S(1)} %copy-done.8), channel_id=1, replica_groups=mesh['parts'=2,'seq'=4,'head'=2,'fsdp'=2] {'seq'}, dimensions={1}, use_global_device_ids=true | all-gather | bytes 655360 | tf_op jit(solution)/shard_map/all_gather | solution.py:77
  170.8 1.4 convolution_convert_fusion
  172.2 0.0 reduce-scatter.5.cloned.1.call-update
  172.2 23.0 %reduce-scatter.5.cloned.1.call-done = bf16[64,1024]{1,0:T(8,128)(2,1)} async-done(((bf16[256,1024]{1,0:T(8,128)(2,1)}), bf16[64,1024]{1,0:T(8,128)(2,1)}) %reduce-scatter.5.cloned.1.call-update) | async-done | bytes 131088 | tf_op jit(solution)/shard_map/reduce_scatter | solution.py:154
  195.2 1.6 add_convert_fusion
  (60 shorter events, 0.4 us)
Async XLA Ops:
  6.5 15.8 %copy-start.3 = (bf16[256,256]{1,0:T(8,128)(2,1)S(1)}, bf16[256,256]{1,0:T(8,128)(2,1)}, u32[]{:S(2)}) copy-start(bf16[256,256]{1,0:T(8,128)(2,1)} %param.19) | copy-start | bytes 393220
  6.5 31.9 %copy-start.4 = (bf16[256,256]{1,0:T(8,128)(2,1)S(1)}, bf16[256,256]{1,0:T(8,128)(2,1)}, u32[]{:S(2)}) copy-start(bf16[256,256]{1,0:T(8,128)(2,1)} %param.20) | copy-start | bytes 393220
  6.5 134.5 %reduce-scatter.3.cloned.1.call-start = ((), (), s32[]{:S(2)}) async-start(), calls=%async_computation.2 | async-start | bytes 655360 | tf_op jit(solution)/shard_map/reduce_scatter | solution.py:132
  6.5 48.1 %collective-permute-start = (bf16[256,256]{1,0:T(8,128)(2,1)}, bf16[256,256]{1,0:T(8,128)(2,1)S(1)}, u32[]{:S(2)}, u32[]{:S(2)}) collective-permute-start(bf16[256,256]{1,0:T(8,128)(2,1)} %param.21), channel_id=1, source_target_pairs={{0,4},{4,8},{8,12},{12,0},{1,5},{5,9},{9,13},{13,1},{2,6},{6,10},{... | collective-permute-start | bytes 393224 | tf_op jit(solution)/shard_map/ppermute | solution.py:17
  9.6 62.6 %collective-permute-start.2 = (bf16[256,256]{1,0:T(8,128)(2,1)}, bf16[256,256]{1,0:T(8,128)(2,1)S(1)}, u32[]{:S(2)}, u32[]{:S(2)}) collective-permute-start(bf16[256,256]{1,0:T(8,128)(2,1)} %param.21), channel_id=1, source_target_pairs={{0,12},{4,0},{8,4},{12,8},{1,13},{5,1},{9,5},{13,9},{2,14},{6,2},{... | collective-permute-start | bytes 393224 | tf_op jit(solution)/shard_map/ppermute | solution.py:19
  14.8 39.8 %copy-start.5 = (bf16[256,256]{1,0:T(8,128)(2,1)S(1)}, bf16[256,256]{1,0:T(8,128)(2,1)}, u32[]{:S(2)}) copy-start(bf16[256,256]{1,0:T(8,128)(2,1)} %param.22) | copy-start | bytes 393220
  38.4 33.7 %copy-start.2 = (bf16[256,256]{1,0:T(8,128)(2,1)S(1)}, bf16[256,256]{1,0:T(8,128)(2,1)}, u32[]{:S(2)}) copy-start(bf16[256,256]{1,0:T(8,128)(2,1)} %param.21) | copy-start | bytes 393220
  54.6 17.5 %collective-permute-start.1 = (bf16[256,256]{1,0:T(8,128)(2,1)S(1)}, bf16[256,256]{1,0:T(8,128)(2,1)S(1)}, u32[]{:S(2)}, u32[]{:S(2)}) collective-permute-start(bf16[256,256]{1,0:T(8,128)(2,1)S(1)} %collective-permute-done), channel_id=1, source_target_pairs={{0,4},{4,8},{8,12},{12,0},{1,5},{5,9},{9,13},{13,1},{2,6},{6,10},{... | collective-permute-start | bytes 393224 | tf_op jit(solution)/shard_map/ppermute | solution.py:17
  108.4 1.9 copy-start.6
  108.5 17.8 %copy-start.7 = (bf16[256,256]{1,0:T(8,128)(2,1)S(1)}, bf16[256,256]{1,0:T(8,128)(2,1)}, u32[]{:S(2)}) copy-start(bf16[256,256]{1,0:T(8,128)(2,1)} %param.24) | copy-start | bytes 393220
  109.6 31.5 %copy-start.9 = (f32[9,256]{1,0:T(8,128)S(1)}, f32[9,256]{1,0:T(8,128)}, u32[]{:S(2)}) copy-start(f32[9,256]{1,0:T(8,128)} %param.26) | copy-start | bytes 27652
  109.6 31.5 %copy-start = (bf16[64,1024]{1,0:T(8,128)(2,1)S(1)}, bf16[64,1024]{1,0:T(8,128)(2,1)}, u32[]{:S(2)}) copy-start(bf16[64,1024]{1,0:T(8,128)(2,1)} %param.16) | copy-start | bytes 393220
  109.6 33.7 %copy-start.10 = (f32[1024]{0:T(1024)S(1)}, f32[1024]{0:T(1024)}, u32[]{:S(2)}) copy-start(f32[1024]{0:T(1024)} %param.23) | copy-start | bytes 12292
  109.6 85.5 %reduce-scatter.5.cloned.1.call-start = ((), (), s32[]{:S(2)}) async-start(), calls=%async_computation.3 | async-start | bytes 655360 | tf_op jit(solution)/shard_map/reduce_scatter | solution.py:154
  151.1 3.0 %copy-start.8 = (bf16[256,256]{1,0:T(8,128)(2,1)S(1)}, bf16[256,256]{1,0:T(8,128)(2,1)}, u32[]{:S(2)}) copy-start(bf16[256,256]{1,0:T(8,128)(2,1)} %param.29) | copy-start | bytes 393220
  151.1 19.6 %copy-start.11 = (f32[256]{0:T(256)S(1)}, f32[256]{0:T(256)}, u32[]{:S(2)}) copy-start(f32[256]{0:T(256)} %param.28) | copy-start | bytes 3076
  151.2 19.6 %copy-start.12 = (f32[256]{0:T(256)S(1)}, f32[256]{0:T(256)}, u32[]{:S(2)}) copy-start(f32[256]{0:T(256)} %param.27) | copy-start | bytes 3076
  151.5 19.2 %collective-permute-start.3 = (bf16[4,256]{1,0:T(4,128)(2,1)S(1)}, bf16[4,256]{1,0:T(4,128)(2,1)S(1)}, u32[]{:S(2)}, u32[]{:S(2)}) collective-permute-start(bf16[4,256]{1,0:T(4,128)(2,1)S(1)} %get-tuple-element.130), channel_id=1, source_target_pairs={{0,4},{4,8},{8,12},{1,5},{5,9},{9,13},{2,6},{6,10},{10,14},{3,7},{... | collective-permute-start | bytes 6152 | tf_op jit(solution)/shard_map/ppermute | solution.py:29
  152.8 17.9 %collective-permute-start.4 = (bf16[4,256]{1,0:T(4,128)(2,1)S(1)}, bf16[4,256]{1,0:T(4,128)(2,1)S(1)}, u32[]{:S(2)}, u32[]{:S(2)}) collective-permute-start(bf16[4,256]{1,0:T(4,128)(2,1)S(1)} %get-tuple-element.131), channel_id=1, source_target_pairs={{4,0},{8,4},{12,8},{5,1},{9,5},{13,9},{6,2},{10,6},{14,10},{7,3},{... | collective-permute-start | bytes 6152 | tf_op jit(solution)/shard_map/ppermute | solution.py:32
  170.8 24.4 %copy-start.1 = (bf16[64,1024]{1,0:T(8,128)(2,1)S(1)}, bf16[64,1024]{1,0:T(8,128)(2,1)}, u32[]{:S(2)}) copy-start(bf16[64,1024]{1,0:T(8,128)(2,1)} %reduce-scatter.3.cloned.1.call-done) | copy-start | bytes 393220
Sparse Core Ops, SparseCore 0:
  109.7 20.2 reduce-scatter.2
  172.3 22.7 reduce-scatter.4
